TPU v7x, 32 devices: a whole 2x2x4 slice. The times are simulated.
32 devices in a mesh: grp: 2 (over x), tile: 16 (over z, y, core).
Axes of the slice: x: 2, y: 2, z: 4, core: 2. Of those that a mesh axis runs over, the one named last changes fastest.
Arguments:
- site_cell: int32 [2048, 2], P(('grp', 'tile')), may hold values from 0 to 63
- site_power: float32 [2048], P(('grp', 'tile')), may hold values from -4.5 to -2
- site_tile: int32 [2048, 1], P(('grp', 'tile')), may hold values from 0 to 15; in each aligned block of 64 rows (0 to 63, 64 to 127, ...) at most 8 rows name the same one
- shadow: bfloat16 [2048, 4096], P(('grp', 'tile')), may hold values from -3.75 to 3.75
Outputs:
- count_dist: float32 [16, 8, 4096], P('tile', None, 'grp')
Inputs may be any that keep to these rules, and one draw needn't show every extreme that they name: `site_tile`: among the 64 sites of one device (aligned blocks of rows), at most 8 name the same tile; in some devices a tile is named by exactly 8.
All inputs are finite; a program needn't handle non-finite values.
Results may differ from a plain program's by a relative error of at most 0.00075.
Values may be sent and summed in bfloat16 or wider, within the bound.
No kernel may reach another device: no remote copies, remote signals or barrier semaphores. Data moves between devices by JAX's collectives and lax.ppermute only.
A program may use at most 64 MiB of HBM per device.

v0:
```python
import jax
import jax.numpy as jnp
from jax import lax
from jax.sharding import PartitionSpec as P

WIN = 64
KMAX = 8


reach_sq = 16.0


def joined(value, axis, join):
    pieces = lax.all_gather(value, axis)
    head = pieces[0]
    tail = pieces[1:]
    so_far, _ = lax.scan(lambda so_far, piece: (join(so_far, piece), None), head, tail)
    return so_far


def convolve(first_dist, second_dist, state_axis):
    count_first = first_dist.shape[state_axis]
    count_second = second_dist.shape[state_axis]
    count_out = min(count_first + count_second - 1, KMAX)
    term_list = []
    for k in range(count_out):
        running = None
        for i in range(max(0, k - count_second + 1), min(k, count_first - 1) + 1):
            product = lax.index_in_dim(
                first_dist, i, state_axis, keepdims=False
            ) * lax.index_in_dim(second_dist, k - i, state_axis, keepdims=False)
            running = product if running is None else running + product
        term_list.append(running)
    return jnp.stack(term_list, state_axis)


def merge_pair(first_dist, second_dist):
    return convolve(first_dist, second_dist, 0)


def fold_slots(slot_probs):
    detect_prob = slot_probs.astype(jnp.float32)
    states = jnp.stack([1.0 - detect_prob, detect_prob], axis=1)
    while states.shape[0] > 1:
        if states.shape[0] % 2:
            count_states = states.shape[1]
            columns = states.shape[2]
            identity = jnp.concatenate(
                [
                    jnp.ones((1, 1, columns), jnp.float32),
                    jnp.zeros((1, count_states - 1, columns), jnp.float32),
                ],
                axis=1,
            )
            states = jnp.concatenate([states, identity], axis=0)
        states = convolve(states[0::2], states[1::2], 1)
    result = states[0]
    if result.shape[0] < KMAX:
        result = jnp.concatenate(
            [result, jnp.zeros((KMAX - result.shape[0], result.shape[1]), jnp.float32)], axis=0
        )
    return result


def fold_columns(slot_probs, block_width):
    slots, columns = slot_probs.shape
    blocks = slot_probs.reshape(slots, columns // block_width, block_width).transpose(1, 0, 2)
    folded = lax.map(fold_slots, blocks)
    return folded.transpose(1, 0, 2).reshape(KMAX, columns)


def site_probs(site_cell, site_power, shadow):
    cell_index = jnp.arange(shadow.shape[1], dtype=jnp.int32)
    cell_row = (cell_index // WIN).astype(jnp.float32)
    cell_col = (cell_index % WIN).astype(jnp.float32)
    row_gap = cell_row[None, :] - site_cell[:, 0:1].astype(jnp.float32)
    col_gap = cell_col[None, :] - site_cell[:, 1:2].astype(jnp.float32)
    margin = (
        site_power[:, None]
        - jnp.log(1.0 + (row_gap * row_gap + col_gap * col_gap) / reach_sq)
        + shadow.astype(jnp.float32)
    )
    return jax.nn.sigmoid(margin).astype(jnp.bfloat16)


def on_device(site_cell, site_power, site_tile, shadow):
    tiles = lax.axis_size("tile")
    groups = lax.axis_size("grp")
    site_count = shadow.shape[0]
    capacity = max(2, 2 * site_count // tiles)
    cells_all = shadow.shape[1]
    width = cells_all // groups
    detect_prob = site_probs(site_cell, site_power, shadow)
    owner_tile = site_tile[:, 0]
    hit_table = (owner_tile[:, None] == jnp.arange(tiles, dtype=jnp.int32)[None, :]).astype(
        jnp.int32
    )
    slot_rank = jnp.sum((jnp.cumsum(hit_table, axis=0) - hit_table) * hit_table, axis=1)
    slot_index = owner_tile * capacity + slot_rank
    selector = (
        slot_index[None, :] == jnp.arange(tiles * capacity, dtype=jnp.int32)[:, None]
    ).astype(jnp.bfloat16)
    outgoing = jnp.dot(selector, detect_prob, preferred_element_type=jnp.float32).astype(
        jnp.bfloat16
    )
    outgoing = outgoing.reshape(tiles * capacity, groups, width)
    items = jnp.moveaxis(
        lax.all_to_all(outgoing, "tile", split_axis=0, concat_axis=0, tiled=True), 1, 0
    )
    folded = lax.map(lambda piece: fold_columns(piece, min(piece.shape[1], 512)), items)
    group_dist = jnp.moveaxis(folded, 0, 1)
    merged = joined(group_dist, "grp", merge_pair)
    own_states = lax.dynamic_index_in_dim(merged, lax.axis_index("grp"), 1, keepdims=False)
    return own_states[None, :, :]


def solution(mesh):
    placed = (
        P(("grp", "tile"), None),
        P(("grp", "tile")),
        P(("grp", "tile"), None),
        P(("grp", "tile"), None),
    )
    return jax.shard_map(
        on_device, mesh=mesh, in_specs=placed, out_specs=P("tile", None, "grp"), check_vma=False
    )
```

profile of v0, /device:TPU:0, one launch (start us, length us, event | category | flops | bytes accessed | tf_op | source)
XLA Modules:
  0.0 91.5 jit_solution(106595305176104086)
XLA Ops:
  0.0 0.7 fusion.24
  0.8 0.8 select_reduce_fusion
  1.7 0.7 multiply_add_fusion.35
  2.3 0.8 convert_bitcast_fusion.1
  3.1 2.0 %convolution_convert_fusion = bf16[128,4096]{1,0:T(8,128)(2,1)S(1)} fusion(bf16[64,4096]{1,0:T(8,128)(2,1)} %param.11, f32[64]{0:T(128)S(1)} %get-tuple-element.135, f32[4096]{0:T(1024)S(1)} %get-tuple-element.137, f32[64]{0:T(128)S(1)} %get-tuple-element.134, f32[4096]{0:T(1024)S(1)} %get-tuple-element.136, f32[64]{0:T(128)} %param.9, ...), kind=kOutput, calls=%fused_computation.71 | convolution fusion | flops 71311360 | bytes 1606656 | tf_op jit(solution)/shard_map/dot_general | solution.py:103
  5.1 1.6 %reshape.1052 = bf16[128,2,2048]{2,1,0:T(2,128)(2,1)} reshape(bf16[128,4096]{1,0:T(8,128)(2,1)S(1)} %convolution_convert_fusion) | data formatting | bytes 2097152 | tf_op jit(solution)/shard_map/reshape | solution.py:106
  6.7 7.4 %all-to-all-start = ((bf16[128,2,2048]{2,1,0:T(2,128)(2,1)}), bf16[128,2,2048]{2,1,0:T(2,128)(2,1)S(1)}, u32[]{:S(2)}, u32[]{:S(2)}) async-start(bf16[128,2,2048]{2,1,0:T(2,128)(2,1)} %reshape.1052), calls=%async_computation | async-start | bytes 2097152 | tf_op jit(solution)/shard_map/all_to_all | solution.py:108
  14.1 22.9 %all-to-all-done = bf16[128,2,2048]{2,1,0:T(2,128)(2,1)S(1)} async-done(((bf16[128,2,2048]{2,1,0:T(2,128)(2,1)}), bf16[128,2,2048]{2,1,0:T(2,128)(2,1)S(1)}, u32[]{:S(2)}, u32[]{:S(2)}) %all-to-all-start) | async-done | bytes 1048608 | tf_op jit(solution)/shard_map/all_to_all | solution.py:108
  37.4 45.9 %while.25 = (s32[]{:T(128)}, f32[2,8,2048]{2,1,0:T(8,128)S(1)}, bf16[2,128,2048]{2,1,0:T(8,128)(2,1)S(1)}, s32[]{:T(128)}, s32[]{:T(128)}, /*index=5*/s32[]{:T(128)}) while((s32[]{:T(128)}, f32[2,8,2048]{2,1,0:T(8,128)S(1)}, bf16[2,128,2048]{2,1,0:T(8,128)(2,1)S(1)}, s32[]{:T(128)}, s32[]{:T(128)}, /*index=5*/s32[]{:T(128)}) %tuple.136), condition=%wide.region_5.6_spmd, body=%wide.region_2.5_spmd.sunk | while | flops 1654788 | bytes 14295218 | solution.py:110
  37.9 22.5 %while.26 = (s32[]{:T(128)}, f32[4,8,512]{2,1,0:T(8,128)S(1)}, bf16[4,128,512]{2,0,1:T(4,128)(2,1)S(1)}, s32[]{:T(128)}) while((s32[]{:T(128)}, f32[4,8,512]{2,1,0:T(8,128)S(1)}, bf16[4,128,512]{2,0,1:T(4,128)(2,1)S(1)}, s32[]{:T(128)}) %tuple.139), condition=%wide.region_4.4_spmd, body=%wide.region_3.3_spmd.sunk | while | flops 1654786 | bytes 12066877 | solution.py:68
  38.3 0.5 pad_maximum_fusion.4
  40.0 0.5 stack.31
  41.3 0.4 stack.32
  43.9 0.5 pad_maximum_fusion.4
  45.6 0.5 stack.31
  46.9 0.4 stack.32
  49.5 0.5 pad_maximum_fusion.4
  51.2 0.5 stack.31
  52.5 0.4 stack.32
  55.1 0.5 pad_maximum_fusion.4
  56.8 0.5 stack.31
  60.8 22.5 %while.26 = (s32[]{:T(128)}, f32[4,8,512]{2,1,0:T(8,128)S(1)}, bf16[4,128,512]{2,0,1:T(4,128)(2,1)S(1)}, s32[]{:T(128)}) while((s32[]{:T(128)}, f32[4,8,512]{2,1,0:T(8,128)S(1)}, bf16[4,128,512]{2,0,1:T(4,128)(2,1)S(1)}, s32[]{:T(128)}) %tuple.139), condition=%wide.region_4.4_spmd, body=%wide.region_3.3_spmd.sunk | while | flops 1654786 | bytes 12066877 | solution.py:68
  61.2 0.5 pad_maximum_fusion.4
  62.9 0.5 stack.31
  66.8 0.5 pad_maximum_fusion.4
  68.5 0.5 stack.31
  72.4 0.5 pad_maximum_fusion.4
  74.1 0.5 stack.31
  78.0 0.5 pad_maximum_fusion.4
  79.7 0.5 stack.31
  83.3 6.7 %all-gather = f32[16,2,2048]{2,0,1:T(8,128)S(1)} all-gather(f32[8,2,2048]{2,0,1:T(8,128)S(1)} %bitcast.234), channel_id=2, replica_groups=mesh['grp'=2,'tile'=16] {'grp'}, dimensions={0}, use_global_device_ids=true | all-gather | bytes 393216 | tf_op jit(solution)/shard_map/all_gather | solution.py:14
  90.9 0.6 dynamic-slice_bitcast_fusion
  (286 shorter events, 35.7 us)
Async XLA Ops:
  6.7 30.3 %all-to-all-start = ((bf16[128,2,2048]{2,1,0:T(2,128)(2,1)}), bf16[128,2,2048]{2,1,0:T(2,128)(2,1)S(1)}, u32[]{:S(2)}, u32[]{:S(2)}) async-start(bf16[128,2,2048]{2,1,0:T(2,128)(2,1)} %reshape.1052), calls=%async_computation | async-start | bytes 2097152 | tf_op jit(solution)/shard_map/all_to_all | solution.py:108
where the time goes:
time: 92.2 us; the launch traced here: 91.5 us
  other arithmetic  34.7 us (38%)
  waiting for transfers between devices  22.9 us (25%)
  local copies, waits for them, and re-layouts  15.6 us (17%)
  starting transfers between devices  7.39 us (8%)
  blocking collectives  6.68 us (7%)
  loops' own time  2.16 us (2%)
  matrix products  2.01 us (2%)
    all_to_all x1, waiting for transfers between devices, on_device(): lax.all_to_all(outgoing, 'tile', split_axis=0, concat_axis=0, tiled=True)  22.9 us
    add x156, other arithmetic, convolve(): running = product if running is None else running + product  16.5 us
    another operation x41, local copies, waits for them, and re-layouts, convolve(): return jnp.stack(term_list, state_axis)  10.5 us
    all_to_all x1, starting transfers between devices, on_device(): lax.all_to_all(outgoing, 'tile', split_axis=0, concat_axis=0, tiled=True)  7.39 us
    all_gather x1, blocking collectives, joined(): pieces = lax.all_gather(value, axis)  6.68 us
    mul x16, other arithmetic, convolve(): lax.index_in_dim(first_dist, i, state_axis, keepdims=False)  5.62 us
    another operation x8, other arithmetic, fold_slots(): states = jnp.stack([1.0 - detect_prob, detect_prob], axis=1)  3.81 us
    sub x8, other arithmetic, fold_slots(): states = jnp.stack([1.0 - detect_prob, detect_prob], axis=1)  2.91 us
  transfers between devices with their start and end apart: 1, of which 1 were waited for; matrix products, arithmetic and copies ran while one was open for 0% of the time, Pallas kernels for 0%

commit v1 on v0

v1 whole, which is shorter than its diff:
```python
import functools

import jax
import jax.numpy as jnp
from jax import lax
from jax.experimental import pallas as pl
from jax.experimental.pallas import tpu as pltpu
from jax.sharding import Mesh, PartitionSpec as P

WIN = 64
KMAX = 8
LANES = 128

reach_sq = 16.0


def column(row_values):
    n = row_values.shape[1]
    on_diagonal = lax.broadcasted_iota(jnp.int32, (n, n), 0) == lax.broadcasted_iota(
        jnp.int32, (n, n), 1
    )
    return jnp.sum(jnp.where(on_diagonal, row_values, 0.0), axis=1, keepdims=True)


def probs_kernel(tiles, cell_ref, power_ref, tile_ref, shadow_ref, out_ref):
    sites = shadow_ref.shape[0]
    receivers = out_ref.shape[0]
    strips = shadow_ref.shape[1] // receivers // LANES
    tile_row = tile_ref[...].astype(jnp.float32)
    before = lax.broadcasted_iota(jnp.int32, (sites, sites), 0) < lax.broadcasted_iota(
        jnp.int32, (sites, sites), 1
    )
    same = column(tile_row) == tile_row
    rank = jnp.sum(jnp.where(same & before, 1.0, 0.0), axis=0, keepdims=True)
    slot = rank * tiles + tile_row
    slot_rows = jnp.broadcast_to(
        jnp.concatenate([slot] * (LANES // sites), axis=1), (8, LANES)
    ).astype(jnp.bfloat16)

    lane = lax.broadcasted_iota(jnp.int32, (sites, LANES), 1)
    cell = cell_ref[...].astype(jnp.float32)
    row_gap = (lane // WIN).astype(jnp.float32) - column(cell[0:1, :])
    col_gap = (lane % WIN).astype(jnp.float32) - column(cell[1:2, :])
    col_part = 1.0 + col_gap * col_gap / reach_sq
    row_quarter = row_gap * 0.25
    power = jnp.broadcast_to(column(power_ref[...]), (sites, LANES))

    for block in range(receivers):
        for strip in range(strips):
            first = (block * strips + strip) * LANES
            window = shadow_ref[:, first : first + LANES].astype(jnp.float32)
            row_part = row_quarter + (first // WIN) * 0.25
            loss = col_part + row_part * row_part
            odds_against = loss * jnp.exp(-(power + window))
            out_ref[block, strip * sites : (strip + 1) * sites, :] = (
                1.0 / (1.0 + odds_against)
            ).astype(jnp.bfloat16)
        out_ref[block, strips * sites : strips * sites + 8, :] = slot_rows


def count_kernel(tiles, capacity, sites, blocks_ref, out_ref, even_ref, odd_ref):
    senders = blocks_ref.shape[0]
    strips = even_ref.shape[1] // LANES
    slots = tiles * capacity
    slot_number = lax.broadcasted_iota(jnp.int32, (slots, sites), 0).astype(jnp.float32)

    def place(sender, slots_ref):
        named = blocks_ref[sender, pl.ds(strips * sites, 8), :].astype(jnp.float32)
        selector = (slot_number == named[0:1, :sites]).astype(jnp.bfloat16)
        for strip in range(strips):
            probs = blocks_ref[sender, strip * sites : (strip + 1) * sites, :]
            slots_ref[:, strip * LANES : (strip + 1) * LANES] = jnp.dot(
                selector, probs, preferred_element_type=jnp.float32
            )

    def add_pair(states, hit_a, hit_b):
        miss_a = 1.0 - hit_a
        miss_b = 1.0 - hit_b
        none = miss_a * miss_b
        both = hit_a * hit_b
        one = (hit_a + hit_b) - (both + both)
        new = []
        for k in range(KMAX):
            term = states[k] * none
            if k >= 1:
                term = term + states[k - 1] * one
            if k >= 2:
                term = term + states[k - 2] * both
            new.append(term)
        return new

    def add_sender(states, slots_ref):
        for rank in range(0, capacity, 2):
            states = add_pair(
                states,
                slots_ref[rank * tiles : (rank + 1) * tiles, :],
                slots_ref[(rank + 1) * tiles : (rank + 2) * tiles, :],
            )
        return states

    width = even_ref.shape[1]
    states = [jnp.ones((tiles, width), jnp.float32)] + [
        jnp.zeros((tiles, width), jnp.float32) for _ in range(KMAX - 1)
    ]
    place(0, even_ref)

    def step(i, states):
        place(2 * i + 1, odd_ref)
        states = add_sender(list(states), even_ref)
        place(jnp.minimum(2 * i + 2, senders - 1), even_ref)
        return tuple(add_sender(states, odd_ref))

    states = lax.fori_loop(0, senders // 2, step, tuple(states))
    for k in range(KMAX):
        for strip in range(strips):
            out_ref[pl.ds(strip * KMAX + k, tiles, stride=strips * KMAX), :] = states[k][
                :, strip * LANES : (strip + 1) * LANES
            ]


def merge_kernel(parts, in_ref, out_ref):
    pieces = in_ref.shape[0] // parts
    strips = in_ref.shape[1] // KMAX
    count = lax.broadcasted_iota(jnp.int32, (KMAX, LANES), 0)
    for piece in range(pieces):
        for strip in range(strips):
            rows = slice(strip * KMAX, (strip + 1) * KMAX)
            total = in_ref[piece, rows, :]
            for part in range(1, parts):
                other = in_ref[part * pieces + piece, rows, :]
                joint = other * total[0:1, :]
                for k in range(1, KMAX):
                    shifted = jnp.where(count >= k, pltpu.roll(other, k, 0), 0.0)
                    joint = joint + shifted * total[k : k + 1, :]
                total = joint
            first = (piece * strips + strip) * LANES
            out_ref[0, :, first : first + LANES] = total


def on_device(site_cell, site_power, site_tile, shadow):
    groups = lax.axis_size("grp")
    parts = lax.axis_size("far")
    near = lax.axis_size("near")
    tiles = parts * near
    sites, cells = shadow.shape
    capacity = max(2, 2 * sites // tiles)
    receivers = groups * near
    width = cells // receivers
    rows = sites * (width // LANES) + 8

    blocks = pl.pallas_call(
        functools.partial(probs_kernel, tiles),
        out_shape=jax.ShapeDtypeStruct((receivers, rows, LANES), jnp.bfloat16),
        name="probs",
    )(site_cell.T, site_power[None, :], site_tile.T, shadow)
    blocks = lax.all_to_all(blocks, ("grp", "near"), split_axis=0, concat_axis=0, tiled=True)
    dist = pl.pallas_call(
        functools.partial(count_kernel, tiles, capacity, sites),
        out_shape=jax.ShapeDtypeStruct((tiles * KMAX * width // LANES, LANES), jnp.float32),
        scratch_shapes=[pltpu.VMEM((tiles * capacity, width), jnp.float32)] * 2,
        name="counts",
    )(blocks)
    dist = dist.reshape(tiles, KMAX * width // LANES, LANES)
    dist = lax.all_to_all(dist, ("far", "near"), split_axis=0, concat_axis=0, tiled=True)
    return pl.pallas_call(
        functools.partial(merge_kernel, parts),
        out_shape=jax.ShapeDtypeStruct((1, KMAX, cells // groups), jnp.float32),
        name="merge",
    )(dist)


def solution(mesh):
    groups, tiles = mesh.shape["grp"], mesh.shape["tile"]
    near = min(tiles // 2, max(1, WIN * WIN // LANES // groups))
    split = Mesh(mesh.devices.reshape(groups, tiles // near, near), ("grp", "far", "near"))
    everywhere = ("grp", "far", "near")
    placed = (P(everywhere, None), P(everywhere), P(everywhere, None), P(everywhere, None))
    return jax.shard_map(
        on_device,
        mesh=split,
        in_specs=placed,
        out_specs=P(("far", "near"), None, "grp"),
        check_vma=False,
    )
```

time: 92.2 us -> 37.7 us (0.41)
  other arithmetic: 34.7 us -> 0 us
  waiting for transfers between devices: 22.9 us -> 0 us
  blocking collectives: 6.68 us -> 29.4 us
  local copies, waits for them, and re-layouts: 15.6 us -> 0 us
  Pallas kernels: 0 us -> 7.89 us
  starting transfers between devices: 7.39 us -> 0 us
  loops' own time: 2.16 us -> 0 us
  matrix products: 2.01 us -> 0 us
    all_to_all x0 -> x2, blocking collectives: none -> 29.4 us  [the longest x1 17.3 us: on_device(): lax.all_to_all(blocks, ('grp', 'near'), split_axis=0, concat_axis=0, tile...]
    all_to_all x1 -> x0, waiting for transfers between devices: 22.9 us -> none  [on_device(): lax.all_to_all(outgoing, 'tile', split_axis=0, concat_axis=0, tiled=True)]
    add x157 -> x0, other arithmetic: 17.2 us -> none  [the longest x156 16.5 us: convolve(): running = product if running is None else running + product]
    another operation x41 -> x0, local copies, waits for them, and re-layouts: 10.5 us -> none  [convolve(): return jnp.stack(term_list, state_axis)]
    pallas_call x0 -> x3, Pallas kernels: none -> 7.89 us  [the longest x1 3.84 us: on_device(): pl.pallas_call(functools.partial(count_kernel, tiles, capacity, sites), o...]
    all_to_all x1 -> x0, starting transfers between devices: 7.39 us -> none  [on_device(): lax.all_to_all(outgoing, 'tile', split_axis=0, concat_axis=0, tiled=True)]
    all_gather x1 -> x0, blocking collectives: 6.68 us -> none  [joined(): pieces = lax.all_gather(value, axis)]
    another operation x19 -> x0, other arithmetic: 6.66 us -> none  [the longest x8 3.81 us: fold_slots(): states = jnp.stack([1.0 - detect_prob, detect_prob], axis=1)]
  transfers between devices with their start and end apart: 1 -> 0, of which waited for: 1 -> 0; matrix products, arithmetic and copies ran while one was open for 0% -> 0% of each run, Pallas kernels for 0% -> 0%
where the time goes in v1:
time: 37.7 us; the launch traced here: 37.3 us
  blocking collectives  29.4 us (78%)
  Pallas kernels  7.89 us (21%)
    all_to_all x1, blocking collectives, on_device(): lax.all_to_all(blocks, ('grp', 'near'), split_axis=0, concat_axis=0, tile...  17.3 us
    all_to_all x1, blocking collectives, on_device(): lax.all_to_all(dist, ('far', 'near'), split_axis=0, concat_axis=0, tiled=...  12.1 us
    pallas_call x1, Pallas kernels, on_device(): pl.pallas_call(functools.partial(count_kernel, tiles, capacity, sites), o...  3.84 us
    pallas_call x1, Pallas kernels, on_device(): pl.pallas_call(functools.partial(probs_kernel, tiles), out_shape=jax.Shap...  2.45 us
    pallas_call x1, Pallas kernels, on_device(): pl.pallas_call(functools.partial(merge_kernel, parts), out_shape=jax.Shap...  1.6 us

profile of v1, /device:TPU:0, one launch (start us, length us, event | category | flops | bytes accessed | tf_op | source)
XLA Modules:
  0.0 37.3 jit_solution(10811285228908670565)
XLA Ops:
  0.0 2.4 %probs.1 = bf16[16,136,128]{2,1,0:T(8,128)(2,1)} custom-call(s32[2,64]{1,0:T(2,128)} %bitcast.5, f32[1,64]{1,0:T(1,128)} %bitcast.6, s32[1,64]{1,0:T(1,128)} %bitcast.7, bf16[64,4096]{1,0:T(8,128)(2,1)} %shadow_ref.1), custom_call_target="tpu_custom_call" | custom-call | tf_op jit(solution)/shard_map/probs/pallas_call | solution.py:151
  2.4 17.3 %all_to_all.10.blocks_ref = bf16[16,136,128]{2,1,0:T(8,128)(2,1)} all-to-all(bf16[16,136,128]{2,1,0:T(8,128)(2,1)} %probs.1), channel_id=1, replica_groups=mesh['grp'=2,'far'=2,'near'=8] {'grp','near'}, dimensions={0} | all-to-all | bytes 1114112 | tf_op jit(solution)/shard_map/all_to_all | solution.py:156
  19.7 3.8 %counts.1 = f32[256,128]{1,0:T(8,128)} custom-call(bf16[16,136,128]{2,1,0:T(8,128)(2,1)} %all_to_all.10.blocks_ref), custom_call_target="tpu_custom_call" | custom-call | tf_op jit(solution)/shard_map/counts/pallas_call | solution.py:157
  23.6 12.1 %all_to_all.11.in_ref = f32[16,16,128]{2,1,0:T(8,128)} all-to-all(f32[16,16,128]{2,1,0:T(8,128)} %bitcast.4), channel_id=1, replica_groups=mesh['grp'=2,'far'=2,'near'=8] {'far','near'}, dimensions={0} | all-to-all | bytes 262144 | tf_op jit(solution)/shard_map/all_to_all | solution.py:164
  35.7 1.6 %merge.1 = f32[1,8,2048]{2,1,0:T(8,128)} custom-call(f32[16,16,128]{2,1,0:T(8,128)} %all_to_all.11.in_ref), custom_call_target="tpu_custom_call" | custom-call | tf_op jit(solution)/shard_map/merge/pallas_call | solution.py:165

commit v2 on v1

--- a/solution.py
+++ b/solution.py
@@ -22,10 +22,30 @@
     return jnp.sum(jnp.where(on_diagonal, row_values, 0.0), axis=1, keepdims=True)
 
 
-def probs_kernel(tiles, cell_ref, power_ref, tile_ref, shadow_ref, out_ref):
+def probs_kernel(
+    tiles, cell_hbm, power_hbm, tile_hbm, shadow_hbm, out_ref, cell_ref, power_ref, tile_ref, shadow_ref, sems
+):
     sites = shadow_ref.shape[0]
     receivers = out_ref.shape[0]
     strips = shadow_ref.shape[1] // receivers // LANES
+    pieces = sems.shape[0] - 3
+    span = shadow_ref.shape[1] // pieces
+    small = [
+        pltpu.make_async_copy(source, target, sems.at[pieces + i])
+        for i, (source, target) in enumerate(
+            [(cell_hbm, cell_ref), (power_hbm, power_ref), (tile_hbm, tile_ref)]
+        )
+    ]
+    windows = []
+    for i in range(pieces):
+        part = slice(i * span, (i + 1) * span)
+        windows.append(
+            pltpu.make_async_copy(shadow_hbm.at[:, part], shadow_ref.at[:, part], sems.at[i])
+        )
+    for copy in small + windows:
+        copy.start()
+    for copy in small:
+        copy.wait()
     tile_row = tile_ref[...].astype(jnp.float32)
     before = lax.broadcasted_iota(jnp.int32, (sites, sites), 0) < lax.broadcasted_iota(
         jnp.int32, (sites, sites), 1
@@ -46,8 +66,11 @@
     power = jnp.broadcast_to(column(power_ref[...]), (sites, LANES))
 
     for block in range(receivers):
+        out_ref[block, strips * sites : strips * sites + 8, :] = slot_rows
         for strip in range(strips):
             first = (block * strips + strip) * LANES
+            if first % span == 0:
+                windows[first // span].wait()
             window = shadow_ref[:, first : first + LANES].astype(jnp.float32)
             row_part = row_quarter + (first // WIN) * 0.25
             loss = col_part + row_part * row_part
@@ -55,7 +78,6 @@
             out_ref[block, strip * sites : (strip + 1) * sites, :] = (
                 1.0 / (1.0 + odds_against)
             ).astype(jnp.bfloat16)
-        out_ref[block, strips * sites : strips * sites + 8, :] = slot_rows
 
 
 def count_kernel(tiles, capacity, sites, blocks_ref, out_ref, even_ref, odd_ref):
@@ -67,11 +89,10 @@
     def place(sender, slots_ref):
         named = blocks_ref[sender, pl.ds(strips * sites, 8), :].astype(jnp.float32)
         selector = (slot_number == named[0:1, :sites]).astype(jnp.bfloat16)
-        for strip in range(strips):
-            probs = blocks_ref[sender, strip * sites : (strip + 1) * sites, :]
-            slots_ref[:, strip * LANES : (strip + 1) * LANES] = jnp.dot(
-                selector, probs, preferred_element_type=jnp.float32
-            )
+        probs = jnp.concatenate(
+            [blocks_ref[sender, i * sites : (i + 1) * sites, :] for i in range(strips)], axis=1
+        )
+        slots_ref[...] = jnp.dot(selector, probs, preferred_element_type=jnp.float32)
 
     def add_pair(states, hit_a, hit_b):
         miss_a = 1.0 - hit_a
@@ -102,15 +123,12 @@
     states = [jnp.ones((tiles, width), jnp.float32)] + [
         jnp.zeros((tiles, width), jnp.float32) for _ in range(KMAX - 1)
     ]
-    place(0, even_ref)
-
-    def step(i, states):
-        place(2 * i + 1, odd_ref)
-        states = add_sender(list(states), even_ref)
-        place(jnp.minimum(2 * i + 2, senders - 1), even_ref)
-        return tuple(add_sender(states, odd_ref))
-
-    states = lax.fori_loop(0, senders // 2, step, tuple(states))
+    refs = [even_ref, odd_ref]
+    place(0, refs[0])
+    for i in range(senders):
+        if i + 1 < senders:
+            place(i + 1, refs[(i + 1) % 2])
+        states = add_sender(states, refs[i % 2])
     for k in range(KMAX):
         for strip in range(strips):
             out_ref[pl.ds(strip * KMAX + k, tiles, stride=strips * KMAX), :] = states[k][
@@ -148,16 +166,30 @@
     width = cells // receivers
     rows = sites * (width // LANES) + 8
 
+    small = pltpu.CompilerParams(vmem_limit_bytes=8 * 1024 * 1024)
     blocks = pl.pallas_call(
         functools.partial(probs_kernel, tiles),
         out_shape=jax.ShapeDtypeStruct((receivers, rows, LANES), jnp.bfloat16),
+        in_specs=[pl.BlockSpec(memory_space=pltpu.HBM)] * 4,
+        scratch_shapes=[
+            pltpu.VMEM((2, sites), jnp.int32),
+            pltpu.VMEM((1, sites), jnp.float32),
+            pltpu.VMEM((1, sites), jnp.int32),
+            pltpu.VMEM((sites, cells), jnp.bfloat16),
+            pltpu.SemaphoreType.DMA((4 + 3,)),
+        ],
+        compiler_params=small,
         name="probs",
-    )(site_cell.T, site_power[None, :], site_tile.T, shadow)
+    )(*[
+        pltpu.with_memory_space_constraint(x, pltpu.HBM)
+        for x in (site_cell.T, site_power[None, :], site_tile.T, shadow)
+    ])
     blocks = lax.all_to_all(blocks, ("grp", "near"), split_axis=0, concat_axis=0, tiled=True)
     dist = pl.pallas_call(
         functools.partial(count_kernel, tiles, capacity, sites),
         out_shape=jax.ShapeDtypeStruct((tiles * KMAX * width // LANES, LANES), jnp.float32),
         scratch_shapes=[pltpu.VMEM((tiles * capacity, width), jnp.float32)] * 2,
+        compiler_params=small,
         name="counts",
     )(blocks)
     dist = dist.reshape(tiles, KMAX * width // LANES, LANES)
@@ -165,6 +197,7 @@
     return pl.pallas_call(
         functools.partial(merge_kernel, parts),
         out_shape=jax.ShapeDtypeStruct((1, KMAX, cells // groups), jnp.float32),
+        compiler_params=small,
         name="merge",
     )(dist)
 

time: 37.7 us -> 32.8 us (0.87)
  Pallas kernels: 7.89 us -> 3.85 us
  blocking collectives: 29.4 us -> 28.7 us
    pallas_call x1, Pallas kernels: 3.84 us -> 1.7 us  [on_device(): pl.pallas_call(functools.partial(count_kernel, tiles, capacity, sites), o...]
    pallas_call x1, Pallas kernels: 2.45 us -> 1.45 us  [on_device(): pl.pallas_call(functools.partial(probs_kernel, tiles), out_shape=jax.Shap...]
    pallas_call x1, Pallas kernels: 1.6 us -> 0.7 us  [on_device(): pl.pallas_call(functools.partial(merge_kernel, parts), out_shape=jax.Shap...]
    all_to_all x1, blocking collectives: 12.1 us -> 11.7 us  [on_device(): lax.all_to_all(dist, ('far', 'near'), split_axis=0, concat_axis=0, tiled=...]
where the time goes in v2:
time: 32.8 us; the launch traced here: 32.6 us
  blocking collectives  28.7 us (88%)
  Pallas kernels  3.85 us (12%)
    all_to_all x1, blocking collectives, on_device(): lax.all_to_all(blocks, ('grp', 'near'), split_axis=0, concat_axis=0, tile...  17 us
    all_to_all x1, blocking collectives, on_device(): lax.all_to_all(dist, ('far', 'near'), split_axis=0, concat_axis=0, tiled=...  11.7 us
    pallas_call x1, Pallas kernels, on_device(): pl.pallas_call(functools.partial(count_kernel, tiles, capacity, sites), o...  1.7 us
    pallas_call x1, Pallas kernels, on_device(): pl.pallas_call(functools.partial(probs_kernel, tiles), out_shape=jax.Shap...  1.45 us
    pallas_call x1, Pallas kernels, on_device(): pl.pallas_call(functools.partial(merge_kernel, parts), out_shape=jax.Shap...  0.7 us

profile of v2, /device:TPU:0, one launch (start us, length us, event | category | flops | bytes accessed | tf_op | source)
XLA Modules:
  0.0 32.6 jit_solution(13460668929940759152)
XLA Ops:
  0.0 1.5 %probs.1 = bf16[16,136,128]{2,1,0:T(8,128)(2,1)S(1)} custom-call(s32[2,64]{1,0:T(2,128)} %bitcast.5, f32[1,64]{1,0:T(1,128)} %bitcast.6, s32[1,64]{1,0:T(1,128)} %bitcast.7, bf16[64,4096]{1,0:T(8,128)(2,1)} %shadow_hbm.1), custom_call_target="tpu_custom_call" | custom-call | tf_op jit(solution)/shard_map/probs/pallas_call | solution.py:170
  1.5 17.0 %all_to_all.10.blocks_ref = bf16[16,136,128]{2,1,0:T(8,128)(2,1)S(1)} all-to-all(bf16[16,136,128]{2,1,0:T(8,128)(2,1)S(1)} %probs.1), channel_id=1, replica_groups=mesh['grp'=2,'far'=2,'near'=8] {'grp','near'}, dimensions={0} | all-to-all | bytes 1114112 | tf_op jit(solution)/shard_map/all_to_all | solution.py:187
  18.5 1.7 %counts.1 = f32[256,128]{1,0:T(8,128)S(1)} custom-call(bf16[16,136,128]{2,1,0:T(8,128)(2,1)S(1)} %all_to_all.10.blocks_ref), custom_call_target="tpu_custom_call" | custom-call | tf_op jit(solution)/shard_map/counts/pallas_call | solution.py:188
  20.2 11.7 %all_to_all.11.in_ref = f32[16,16,128]{2,1,0:T(8,128)S(1)} all-to-all(f32[16,16,128]{2,1,0:T(8,128)S(1)} %bitcast.4), channel_id=1, replica_groups=mesh['grp'=2,'far'=2,'near'=8] {'far','near'}, dimensions={0} | all-to-all | bytes 262144 | tf_op jit(solution)/shard_map/all_to_all | solution.py:196
  31.9 0.7 %merge.1 = f32[1,8,2048]{2,1,0:T(8,128)} custom-call(f32[16,16,128]{2,1,0:T(8,128)S(1)} %all_to_all.11.in_ref), custom_call_target="tpu_custom_call" | custom-call | tf_op jit(solution)/shard_map/merge/pallas_call | solution.py:197

commit v3 on v2

--- a/solution.py
+++ b/solution.py
@@ -23,7 +23,7 @@
 
 
 def probs_kernel(
-    tiles, cell_hbm, power_hbm, tile_hbm, shadow_hbm, out_ref, cell_ref, power_ref, tile_ref, shadow_ref, sems
+    tiles, half_slots, cell_hbm, power_hbm, tile_hbm, shadow_hbm, out_ref, cell_ref, power_ref, tile_ref, shadow_ref, sems
 ):
     sites = shadow_ref.shape[0]
     receivers = out_ref.shape[0]
@@ -52,7 +52,9 @@
     )
     same = column(tile_row) == tile_row
     rank = jnp.sum(jnp.where(same & before, 1.0, 0.0), axis=0, keepdims=True)
-    slot = rank * tiles + tile_row
+    core = tile_row - 2.0 * jnp.floor(tile_row * 0.5)
+    chip = (tile_row - core) * 0.5
+    slot = core * half_slots + rank * (tiles // 2) + chip
     slot_rows = jnp.broadcast_to(
         jnp.concatenate([slot] * (LANES // sites), axis=1), (8, LANES)
     ).astype(jnp.bfloat16)
@@ -80,60 +82,76 @@
             ).astype(jnp.bfloat16)
 
 
-def count_kernel(tiles, capacity, sites, blocks_ref, out_ref, even_ref, odd_ref):
+def join_pair(states, hit_a, hit_b):
+    miss_a = 1.0 - hit_a
+    miss_b = 1.0 - hit_b
+    none = miss_a * miss_b
+    both = hit_a * hit_b
+    one = (hit_a + hit_b) - (both + both)
+    new = []
+    for k in range(KMAX):
+        term = states[k] * none
+        if k >= 1:
+            term = term + states[k - 1] * one
+        if k >= 2:
+            term = term + states[k - 2] * both
+        new.append(term)
+    return new
+
+
+def count_kernel(for_partner, rows, capacity, sites, blocks_ref, out_ref, *slots_refs):
     senders = blocks_ref.shape[0]
-    strips = even_ref.shape[1] // LANES
-    slots = tiles * capacity
-    slot_number = lax.broadcasted_iota(jnp.int32, (slots, sites), 0).astype(jnp.float32)
+    width = slots_refs[0].shape[1]
+    strips = width // LANES
+    slots = rows * capacity
+    core = lax.axis_index("core")
+    half = 1 - core if for_partner else core
+    first_slot = (half * slots).astype(jnp.float32)
+    slot_number = lax.broadcasted_iota(jnp.int32, (slots, sites), 0).astype(jnp.float32) + first_slot
 
     def place(sender, slots_ref):
-        named = blocks_ref[sender, pl.ds(strips * sites, 8), :].astype(jnp.float32)
+        named = blocks_ref[sender, strips * sites : strips * sites + 8, :].astype(jnp.float32)
         selector = (slot_number == named[0:1, :sites]).astype(jnp.bfloat16)
         probs = jnp.concatenate(
             [blocks_ref[sender, i * sites : (i + 1) * sites, :] for i in range(strips)], axis=1
         )
         slots_ref[...] = jnp.dot(selector, probs, preferred_element_type=jnp.float32)
 
-    def add_pair(states, hit_a, hit_b):
-        miss_a = 1.0 - hit_a
-        miss_b = 1.0 - hit_b
-        none = miss_a * miss_b
-        both = hit_a * hit_b
-        one = (hit_a + hit_b) - (both + both)
-        new = []
-        for k in range(KMAX):
-            term = states[k] * none
-            if k >= 1:
-                term = term + states[k - 1] * one
-            if k >= 2:
-                term = term + states[k - 2] * both
-            new.append(term)
-        return new
-
-    def add_sender(states, slots_ref):
+    states = [jnp.ones((rows, width), jnp.float32)] + [
+        jnp.zeros((rows, width), jnp.float32) for _ in range(KMAX - 1)
+    ]
+    ahead = len(slots_refs)
+    for sender in range(min(ahead, senders)):
+        place(sender, slots_refs[sender])
+    for sender in range(senders):
+        slots_ref = slots_refs[sender % ahead]
         for rank in range(0, capacity, 2):
-            states = add_pair(
+            states = join_pair(
                 states,
-                slots_ref[rank * tiles : (rank + 1) * tiles, :],
-                slots_ref[(rank + 1) * tiles : (rank + 2) * tiles, :],
+                slots_ref[rank * rows : (rank + 1) * rows, :],
+                slots_ref[(rank + 1) * rows : (rank + 2) * rows, :],
             )
-        return states
-
-    width = even_ref.shape[1]
-    states = [jnp.ones((tiles, width), jnp.float32)] + [
-        jnp.zeros((tiles, width), jnp.float32) for _ in range(KMAX - 1)
-    ]
-    refs = [even_ref, odd_ref]
-    place(0, refs[0])
-    for i in range(senders):
-        if i + 1 < senders:
-            place(i + 1, refs[(i + 1) % 2])
-        states = add_sender(states, refs[i % 2])
+        if sender + ahead < senders:
+            place(sender + ahead, slots_ref)
     for k in range(KMAX):
         for strip in range(strips):
-            out_ref[pl.ds(strip * KMAX + k, tiles, stride=strips * KMAX), :] = states[k][
-                :, strip * LANES : (strip + 1) * LANES
-            ]
+            first = (strip * KMAX + k) * rows
+            out_ref[first : first + rows, :] = states[k][:, strip * LANES : (strip + 1) * LANES]
+
+
+def join_kernel(rows, own_ref, got_ref, out_ref):
+    strips = own_ref.shape[0] // (KMAX * rows)
+    for strip in range(strips):
+        parts = []
+        for ref in (own_ref, got_ref):
+            firsts = [(strip * KMAX + k) * rows for k in range(KMAX)]
+            parts.append([ref[first : first + rows, :] for first in firsts])
+        own, got = parts
+        for k in range(KMAX):
+            term = own[0] * got[k]
+            for i in range(1, k + 1):
+                term = term + own[i] * got[k - i]
+            out_ref[pl.ds(strip * KMAX + k, rows, stride=strips * KMAX), :] = term
 
 
 def merge_kernel(parts, in_ref, out_ref):
@@ -159,16 +177,18 @@
     groups = lax.axis_size("grp")
     parts = lax.axis_size("far")
     near = lax.axis_size("near")
-    tiles = parts * near
+    cores = lax.axis_size("core")
+    chips = parts * near
+    tiles = chips * cores
     sites, cells = shadow.shape
     capacity = max(2, 2 * sites // tiles)
     receivers = groups * near
     width = cells // receivers
     rows = sites * (width // LANES) + 8
-
     small = pltpu.CompilerParams(vmem_limit_bytes=8 * 1024 * 1024)
+
     blocks = pl.pallas_call(
-        functools.partial(probs_kernel, tiles),
+        functools.partial(probs_kernel, tiles, chips * capacity),
         out_shape=jax.ShapeDtypeStruct((receivers, rows, LANES), jnp.bfloat16),
         in_specs=[pl.BlockSpec(memory_space=pltpu.HBM)] * 4,
         scratch_shapes=[
@@ -180,19 +200,36 @@
         ],
         compiler_params=small,
         name="probs",
-    )(*[
-        pltpu.with_memory_space_constraint(x, pltpu.HBM)
-        for x in (site_cell.T, site_power[None, :], site_tile.T, shadow)
-    ])
+    )(
+        *[
+            pltpu.with_memory_space_constraint(x, pltpu.HBM)
+            for x in (site_cell.T, site_power[None, :], site_tile.T, shadow)
+        ]
+    )
     blocks = lax.all_to_all(blocks, ("grp", "near"), split_axis=0, concat_axis=0, tiled=True)
+
+    dist_shape = (chips * KMAX * width // LANES, LANES)
+    work = chips * width * receivers * capacity * 23
+
+    def counts(for_partner):
+        return pl.pallas_call(
+            functools.partial(count_kernel, for_partner, chips, capacity, sites),
+            out_shape=jax.ShapeDtypeStruct(dist_shape, jnp.float32),
+            scratch_shapes=[pltpu.VMEM((chips * capacity, width), jnp.float32)] * 2,
+            compiler_params=small,
+            cost_estimate=pl.CostEstimate(flops=work, bytes_accessed=4 * work // 23, transcendentals=0),
+            name="counts_partner" if for_partner else "counts_own",
+        )(blocks)
+
+    swap = [(i, i ^ 1) for i in range(cores)]
+    got = lax.ppermute(counts(True), "core", swap)
     dist = pl.pallas_call(
-        functools.partial(count_kernel, tiles, capacity, sites),
-        out_shape=jax.ShapeDtypeStruct((tiles * KMAX * width // LANES, LANES), jnp.float32),
-        scratch_shapes=[pltpu.VMEM((tiles * capacity, width), jnp.float32)] * 2,
+        functools.partial(join_kernel, chips),
+        out_shape=jax.ShapeDtypeStruct(dist_shape, jnp.float32),
         compiler_params=small,
-        name="counts",
-    )(blocks)
-    dist = dist.reshape(tiles, KMAX * width // LANES, LANES)
+        name="join",
+    )(counts(False), got)
+    dist = dist.reshape(chips, KMAX * width // LANES, LANES)
     dist = lax.all_to_all(dist, ("far", "near"), split_axis=0, concat_axis=0, tiled=True)
     return pl.pallas_call(
         functools.partial(merge_kernel, parts),
@@ -204,14 +241,14 @@
 
 def solution(mesh):
     groups, tiles = mesh.shape["grp"], mesh.shape["tile"]
-    near = min(tiles // 2, max(1, WIN * WIN // LANES // groups))
-    split = Mesh(mesh.devices.reshape(groups, tiles // near, near), ("grp", "far", "near"))
-    everywhere = ("grp", "far", "near")
-    placed = (P(everywhere, None), P(everywhere), P(everywhere, None), P(everywhere, None))
+    near = max(1, min(tiles // 4, WIN * WIN // LANES // groups))
+    names = ("grp", "far", "near", "core")
+    split = Mesh(mesh.devices.reshape(groups, tiles // (2 * near), near, 2), names)
+    placed = (P(names, None), P(names), P(names, None), P(names, None))
     return jax.shard_map(
         on_device,
         mesh=split,
         in_specs=placed,
-        out_specs=P(("far", "near"), None, "grp"),
+        out_specs=P(("far", "near", "core"), None, "grp"),
         check_vma=False,
     )

time: 32.8 us -> 31.7 us (0.966)
  blocking collectives: 28.7 us -> 27 us
  waiting for transfers between devices: 0 us -> 0.5 us
    all_to_all x1, blocking collectives: 17 us -> 15.9 us  [on_device(): lax.all_to_all(blocks, ('grp', 'near'), split_axis=0, concat_axis=0, tile...]
    all_to_all x1, blocking collectives: 11.7 us -> 11.1 us  [on_device(): lax.all_to_all(dist, ('far', 'near'), split_axis=0, concat_axis=0, tiled=...]
    ppermute x0 -> x1, waiting for transfers between devices: none -> 0.5 us  [on_device(): got = lax.ppermute(counts(True), 'core', swap)]
    pallas_call x2 -> x4, Pallas kernels: 3.15 us -> 3.19 us  [the longest x2 1.66 us: counts(): pl.pallas_call(functools.partial(count_kernel, for_partner, chips, capaci...]
  transfers between devices with their start and end apart: 0 -> 1, of which waited for: 0 -> 1; matrix products, arithmetic and copies ran while one was open for 0% -> 0% of each run, Pallas kernels for 0% -> 3%
where the time goes in v3:
time: 31.7 us; the launch traced here: 31.5 us
  blocking collectives  27 us (85%)
  Pallas kernels  3.89 us (12%)
  waiting for transfers between devices  0.5 us (2%)
    all_to_all x1, blocking collectives, on_device(): lax.all_to_all(blocks, ('grp', 'near'), split_axis=0, concat_axis=0, tile...  15.9 us
    all_to_all x1, blocking collectives, on_device(): lax.all_to_all(dist, ('far', 'near'), split_axis=0, concat_axis=0, tiled=...  11.1 us
    pallas_call x2, Pallas kernels, counts(): pl.pallas_call(functools.partial(count_kernel, for_partner, chips, capaci...  1.66 us
    pallas_call x1, Pallas kernels, on_device(): pl.pallas_call(functools.partial(probs_kernel, tiles, chips * capacity),...  1.45 us
    pallas_call x1, Pallas kernels, on_device(): pl.pallas_call(functools.partial(merge_kernel, parts), out_shape=jax.Shap...  0.7 us
  transfers between devices with their start and end apart: 1, of which 1 were waited for; matrix products, arithmetic and copies ran while one was open for 0% of the time, Pallas kernels for 3%

profile of v3, /device:TPU:0, one launch (start us, length us, event | category | flops | bytes accessed | tf_op | source)
XLA Modules:
  0.0 31.5 jit_solution(961621927496850764)
XLA Ops:
  0.0 1.5 %probs.1 = bf16[8,264,128]{2,1,0:T(8,128)(2,1)S(1)} custom-call(s32[2,64]{1,0:T(2,128)} %bitcast.5, f32[1,64]{1,0:T(1,128)} %bitcast.6, s32[1,64]{1,0:T(1,128)} %bitcast.7, bf16[64,4096]{1,0:T(8,128)(2,1)} %shadow_hbm.1), custom_call_target="tpu_custom_call" | custom-call | tf_op jit(solution)/shard_map/probs/pallas_call | solution.py:190
  1.5 15.9 %all_to_all.10.blocks_ref = bf16[8,264,128]{2,1,0:T(8,128)(2,1)S(1)} all-to-all(bf16[8,264,128]{2,1,0:T(8,128)(2,1)S(1)} %probs.1), channel_id=1, replica_groups=mesh['grp'=2,'far'=2,'near'=4,'core'=2] {'grp','near'}, dimensions={0} | all-to-all | bytes 1081344 | tf_op jit(solution)/shard_map/all_to_all | solution.py:209
  17.4 0.8 %counts_partner.1 = f32[256,128]{1,0:T(8,128)S(1)} custom-call(bf16[8,264,128]{2,1,0:T(8,128)(2,1)S(1)} %all_to_all.10.blocks_ref), custom_call_target="tpu_custom_call" | custom-call | flops 6029312 | bytes 1048576 | tf_op jit(solution)/shard_map/counts_partner/pallas_call | solution.py:215
  18.2 0.1 collective-permute-start
  18.3 0.8 %counts_own.1.own_ref = f32[256,128]{1,0:T(8,128)S(1)} custom-call(bf16[8,264,128]{2,1,0:T(8,128)(2,1)S(1)} %all_to_all.10.blocks_ref), custom_call_target="tpu_custom_call" | custom-call | flops 6029312 | bytes 1048576 | tf_op jit(solution)/shard_map/counts_own/pallas_call | solution.py:215
  19.1 0.5 %collective-permute-done.got_ref = f32[256,128]{1,0:T(8,128)S(1)} collective-permute-done((f32[256,128]{1,0:T(8,128)S(1)}, f32[256,128]{1,0:T(8,128)S(1)}, u32[]{:S(2)}, u32[]{:S(2)}) %collective-permute-start) | collective-permute-done | bytes 131104 | tf_op jit(solution)/shard_map/ppermute | solution.py:225
  19.6 0.1 join.1
  19.7 11.1 %all_to_all.11.in_ref = f32[8,32,128]{2,1,0:T(8,128)S(1)} all-to-all(f32[8,32,128]{2,1,0:T(8,128)S(1)} %bitcast.4), channel_id=1, replica_groups=mesh['grp'=2,'far'=2,'near'=4,'core'=2] {'far','near'}, dimensions={0} | all-to-all | bytes 262144 | tf_op jit(solution)/shard_map/all_to_all | solution.py:233
  30.8 0.7 %merge.1 = f32[1,8,2048]{2,1,0:T(8,128)} custom-call(f32[8,32,128]{2,1,0:T(8,128)S(1)} %all_to_all.11.in_ref), custom_call_target="tpu_custom_call" | custom-call | tf_op jit(solution)/shard_map/merge/pallas_call | solution.py:234
Async XLA Ops:
  18.2 1.4 %collective-permute-start = (f32[256,128]{1,0:T(8,128)S(1)}, f32[256,128]{1,0:T(8,128)S(1)}, u32[]{:S(2)}, u32[]{:S(2)}) collective-permute-start(f32[256,128]{1,0:T(8,128)S(1)} %counts_partner.1), channel_id=1, source_target_pairs={{0,1},{1,0},{2,3},{3,2},{4,5},{5,4},{6,7},{7,6},{8,9},{9,8},{10,11... | collective-permute-start | bytes 393224 | tf_op jit(solution)/shard_map/ppermute | solution.py:225

commit v4 on v3

--- a/solution.py
+++ b/solution.py
@@ -12,6 +12,7 @@
 LANES = 128
 
 reach_sq = 16.0
+LOG2E = 1.4426950408889634
 
 
 def column(row_values):
@@ -63,9 +64,11 @@
     cell = cell_ref[...].astype(jnp.float32)
     row_gap = (lane // WIN).astype(jnp.float32) - column(cell[0:1, :])
     col_gap = (lane % WIN).astype(jnp.float32) - column(cell[1:2, :])
-    col_part = 1.0 + col_gap * col_gap / reach_sq
-    row_quarter = row_gap * 0.25
-    power = jnp.broadcast_to(column(power_ref[...]), (sites, LANES))
+    loss = 1.0 + (row_gap * row_gap + col_gap * col_gap) * (1.0 / reach_sq)
+    rise = LANES // WIN
+    step = (2.0 * rise * row_gap + rise * rise) * (1.0 / reach_sq)
+    step_rise = 2.0 * rise * rise / reach_sq
+    power = jnp.broadcast_to(column(power_ref[...]) * -LOG2E, (sites, LANES))
 
     for block in range(receivers):
         out_ref[block, strips * sites : strips * sites + 8, :] = slot_rows
@@ -74,12 +77,12 @@
             if first % span == 0:
                 windows[first // span].wait()
             window = shadow_ref[:, first : first + LANES].astype(jnp.float32)
-            row_part = row_quarter + (first // WIN) * 0.25
-            loss = col_part + row_part * row_part
-            odds_against = loss * jnp.exp(-(power + window))
+            odds_against = loss * jnp.exp2(power - window * LOG2E)
             out_ref[block, strip * sites : (strip + 1) * sites, :] = (
                 1.0 / (1.0 + odds_against)
             ).astype(jnp.bfloat16)
+            loss = loss + step
+            step = step + step_rise
 
 
 def join_pair(states, hit_a, hit_b):
@@ -88,25 +91,24 @@
     none = miss_a * miss_b
     both = hit_a * hit_b
     one = (hit_a + hit_b) - (both + both)
+    if states is None:
+        return [none, one, both]
     new = []
-    for k in range(KMAX):
-        term = states[k] * none
-        if k >= 1:
-            term = term + states[k - 1] * one
-        if k >= 2:
-            term = term + states[k - 2] * both
-        new.append(term)
+    for k in range(min(len(states) + 2, KMAX)):
+        terms = [
+            states[k - i] * factor
+            for i, factor in enumerate((none, one, both))
+            if 0 <= k - i < len(states)
+        ]
+        new.append(functools.reduce(jnp.add, terms))
     return new
 
 
-def count_kernel(for_partner, rows, capacity, sites, blocks_ref, out_ref, *slots_refs):
-    senders = blocks_ref.shape[0]
-    width = slots_refs[0].shape[1]
+def count_sites(states, half, senders, capacity, sites, blocks_ref, slots_refs):
+    slots, width = slots_refs[0].shape
+    rows = slots // capacity
     strips = width // LANES
-    slots = rows * capacity
-    core = lax.axis_index("core")
-    half = 1 - core if for_partner else core
-    first_slot = (half * slots).astype(jnp.float32)
+    first_slot = jnp.asarray(half * slots).astype(jnp.float32)
     slot_number = lax.broadcasted_iota(jnp.int32, (slots, sites), 0).astype(jnp.float32) + first_slot
 
     def place(sender, slots_ref):
@@ -117,11 +119,8 @@
         )
         slots_ref[...] = jnp.dot(selector, probs, preferred_element_type=jnp.float32)
 
-    states = [jnp.ones((rows, width), jnp.float32)] + [
-        jnp.zeros((rows, width), jnp.float32) for _ in range(KMAX - 1)
-    ]
-    ahead = len(slots_refs)
-    for sender in range(min(ahead, senders)):
+    ahead = min(len(slots_refs), senders)
+    for sender in range(ahead):
         place(sender, slots_refs[sender])
     for sender in range(senders):
         slots_ref = slots_refs[sender % ahead]
@@ -133,20 +132,38 @@
             )
         if sender + ahead < senders:
             place(sender + ahead, slots_ref)
+    return states
+
+
+def keep_states(states, dist_ref):
+    rows, width = states[0].shape
     for k in range(KMAX):
-        for strip in range(strips):
+        for strip in range(width // LANES):
             first = (strip * KMAX + k) * rows
-            out_ref[first : first + rows, :] = states[k][:, strip * LANES : (strip + 1) * LANES]
+            dist_ref[first : first + rows, :] = (
+                states[k][:, strip * LANES : (strip + 1) * LANES]
+                if k < len(states)
+                else jnp.zeros((rows, LANES), jnp.float32)
+            )
+
+
+def strip_states(dist_ref, rows, strip):
+    firsts = [(strip * KMAX + k) * rows for k in range(KMAX)]
+    return [dist_ref[first : first + rows, :] for first in firsts]
+
+
+def count_kernel(for_partner, capacity, sites, blocks_ref, out_ref, *slots_refs):
+    core = lax.axis_index("core")
+    half = 1 - core if for_partner else core
+    senders = blocks_ref.shape[0]
+    keep_states(count_sites(None, half, senders, capacity, sites, blocks_ref, slots_refs), out_ref)
 
 
 def join_kernel(rows, own_ref, got_ref, out_ref):
     strips = own_ref.shape[0] // (KMAX * rows)
     for strip in range(strips):
-        parts = []
-        for ref in (own_ref, got_ref):
-            firsts = [(strip * KMAX + k) * rows for k in range(KMAX)]
-            parts.append([ref[first : first + rows, :] for first in firsts])
-        own, got = parts
+        own = strip_states(own_ref, rows, strip)
+        got = strip_states(got_ref, rows, strip)
         for k in range(KMAX):
             term = own[0] * got[k]
             for i in range(1, k + 1):
@@ -177,9 +194,8 @@
     groups = lax.axis_size("grp")
     parts = lax.axis_size("far")
     near = lax.axis_size("near")
-    cores = lax.axis_size("core")
     chips = parts * near
-    tiles = chips * cores
+    tiles = chips * lax.axis_size("core")
     sites, cells = shadow.shape
     capacity = max(2, 2 * sites // tiles)
     receivers = groups * near
@@ -213,7 +229,7 @@
 
     def counts(for_partner):
         return pl.pallas_call(
-            functools.partial(count_kernel, for_partner, chips, capacity, sites),
+            functools.partial(count_kernel, for_partner, capacity, sites),
             out_shape=jax.ShapeDtypeStruct(dist_shape, jnp.float32),
             scratch_shapes=[pltpu.VMEM((chips * capacity, width), jnp.float32)] * 2,
             compiler_params=small,
@@ -221,7 +237,7 @@
             name="counts_partner" if for_partner else "counts_own",
         )(blocks)
 
-    swap = [(i, i ^ 1) for i in range(cores)]
+    swap = [(i, i ^ 1) for i in range(2)]
     got = lax.ppermute(counts(True), "core", swap)
     dist = pl.pallas_call(
         functools.partial(join_kernel, chips),

time: 31.7 us -> 31.7 us (level)
  no operation moved by 1% of the time
where the time goes in v4:
time: 31.7 us; the launch traced here: 31.4 us
  blocking collectives  27 us (85%)
  Pallas kernels  3.81 us (12%)
  waiting for transfers between devices  0.51 us (2%)
    all_to_all x1, blocking collectives, on_device(): lax.all_to_all(blocks, ('grp', 'near'), split_axis=0, concat_axis=0, tile...  15.9 us
    all_to_all x1, blocking collectives, on_device(): lax.all_to_all(dist, ('far', 'near'), split_axis=0, concat_axis=0, tiled=...  11.1 us
    pallas_call x2, Pallas kernels, counts(): pl.pallas_call(functools.partial(count_kernel, for_partner, capacity, sit...  1.62 us
    pallas_call x1, Pallas kernels, on_device(): pl.pallas_call(functools.partial(probs_kernel, tiles, chips * capacity),...  1.42 us
    pallas_call x1, Pallas kernels, on_device(): pl.pallas_call(functools.partial(merge_kernel, parts), out_shape=jax.Shap...  0.7 us
  transfers between devices with their start and end apart: 1, of which 1 were waited for; matrix products, arithmetic and copies ran while one was open for 0% of the time, Pallas kernels for 3%

profile of v4, /device:TPU:0, one launch (start us, length us, event | category | flops | bytes accessed | tf_op | source)
XLA Modules:
  0.0 31.4 jit_solution(6294326488167022359)
XLA Ops:
  0.0 1.4 %probs.1 = bf16[8,264,128]{2,1,0:T(8,128)(2,1)S(1)} custom-call(s32[2,64]{1,0:T(2,128)} %bitcast.5, f32[1,64]{1,0:T(1,128)} %bitcast.6, s32[1,64]{1,0:T(1,128)} %bitcast.7, bf16[64,4096]{1,0:T(8,128)(2,1)} %shadow_hbm.1), custom_call_target="tpu_custom_call" | custom-call | tf_op jit(solution)/shard_map/probs/pallas_call | solution.py:206
  1.4 15.9 %all_to_all.10.blocks_ref = bf16[8,264,128]{2,1,0:T(8,128)(2,1)S(1)} all-to-all(bf16[8,264,128]{2,1,0:T(8,128)(2,1)S(1)} %probs.1), channel_id=1, replica_groups=mesh['grp'=2,'far'=2,'near'=4,'core'=2] {'grp','near'}, dimensions={0} | all-to-all | bytes 1081344 | tf_op jit(solution)/shard_map/all_to_all | solution.py:225
  17.4 0.8 %counts_partner.1 = f32[256,128]{1,0:T(8,128)S(1)} custom-call(bf16[8,264,128]{2,1,0:T(8,128)(2,1)S(1)} %all_to_all.10.blocks_ref), custom_call_target="tpu_custom_call" | custom-call | flops 6029312 | bytes 1048576 | tf_op jit(solution)/shard_map/counts_partner/pallas_call | solution.py:231
  18.2 0.1 collective-permute-start
  18.2 0.8 %counts_own.1.own_ref = f32[256,128]{1,0:T(8,128)S(1)} custom-call(bf16[8,264,128]{2,1,0:T(8,128)(2,1)S(1)} %all_to_all.10.blocks_ref), custom_call_target="tpu_custom_call" | custom-call | flops 6029312 | bytes 1048576 | tf_op jit(solution)/shard_map/counts_own/pallas_call | solution.py:231
  19.1 0.5 %collective-permute-done.got_ref = f32[256,128]{1,0:T(8,128)S(1)} collective-permute-done((f32[256,128]{1,0:T(8,128)S(1)}, f32[256,128]{1,0:T(8,128)S(1)}, u32[]{:S(2)}, u32[]{:S(2)}) %collective-permute-start) | collective-permute-done | bytes 131104 | tf_op jit(solution)/shard_map/ppermute | solution.py:241
  19.6 0.1 join.1
  19.7 11.1 %all_to_all.11.in_ref = f32[8,32,128]{2,1,0:T(8,128)S(1)} all-to-all(f32[8,32,128]{2,1,0:T(8,128)S(1)} %bitcast.4), channel_id=1, replica_groups=mesh['grp'=2,'far'=2,'near'=4,'core'=2] {'far','near'}, dimensions={0} | all-to-all | bytes 262144 | tf_op jit(solution)/shard_map/all_to_all | solution.py:249
  30.7 0.7 %merge.1 = f32[1,8,2048]{2,1,0:T(8,128)} custom-call(f32[8,32,128]{2,1,0:T(8,128)S(1)} %all_to_all.11.in_ref), custom_call_target="tpu_custom_call" | custom-call | tf_op jit(solution)/shard_map/merge/pallas_call | solution.py:250
Async XLA Ops:
  18.2 1.4 %collective-permute-start = (f32[256,128]{1,0:T(8,128)S(1)}, f32[256,128]{1,0:T(8,128)S(1)}, u32[]{:S(2)}, u32[]{:S(2)}) collective-permute-start(f32[256,128]{1,0:T(8,128)S(1)} %counts_partner.1), channel_id=1, source_target_pairs={{0,1},{1,0},{2,3},{3,2},{4,5},{5,4},{6,7},{7,6},{8,9},{9,8},{10,11... | collective-permute-start | bytes 393224 | tf_op jit(solution)/shard_map/ppermute | solution.py:241

commit v5 on v4

--- a/solution.py
+++ b/solution.py
@@ -13,6 +13,26 @@
 
 reach_sq = 16.0
 LOG2E = 1.4426950408889634
+
+
+def swapped_chips(chips):
+    return chips // 2
+
+
+def backwards(count):
+    return list(range(count))[::-1]
+
+
+def gray_backwards(count):
+    return [i ^ (i >> 1) for i in range(count)][::-1]
+
+
+gather_order = backwards
+exchange_order = gray_backwards
+
+
+def places(order):
+    return [order.index(member) for member in range(len(order))]
 
 
 def column(row_values):
@@ -55,7 +75,12 @@
     rank = jnp.sum(jnp.where(same & before, 1.0, 0.0), axis=0, keepdims=True)
     core = tile_row - 2.0 * jnp.floor(tile_row * 0.5)
     chip = (tile_row - core) * 0.5
-    slot = core * half_slots + rank * (tiles // 2) + chip
+    swapped = jnp.where(chip < swapped_chips(tiles // 2), 1.0, 0.0)
+    half = core + swapped - 2.0 * core * swapped
+    place = jnp.zeros_like(chip)
+    for number, where in enumerate(places(exchange_order(tiles // 2))):
+        place = jnp.where(chip == number, float(where), place)
+    slot = half * half_slots + rank * (tiles // 2) + place
     slot_rows = jnp.broadcast_to(
         jnp.concatenate([slot] * (LANES // sites), axis=1), (8, LANES)
     ).astype(jnp.bfloat16)
@@ -70,10 +95,10 @@
     step_rise = 2.0 * rise * rise / reach_sq
     power = jnp.broadcast_to(column(power_ref[...]) * -LOG2E, (sites, LANES))
 
-    for block in range(receivers):
+    for chunk, block in enumerate(places(gather_order(receivers))):
         out_ref[block, strips * sites : strips * sites + 8, :] = slot_rows
         for strip in range(strips):
-            first = (block * strips + strip) * LANES
+            first = (chunk * strips + strip) * LANES
             if first % span == 0:
                 windows[first // span].wait()
             window = shadow_ref[:, first : first + LANES].astype(jnp.float32)
@@ -153,8 +178,10 @@
 
 
 def count_kernel(for_partner, capacity, sites, blocks_ref, out_ref, *slots_refs):
-    core = lax.axis_index("core")
-    half = 1 - core if for_partner else core
+    rows = slots_refs[0].shape[0] // capacity
+    chip = lax.axis_index("far") * lax.axis_size("near") + lax.axis_index("near")
+    swapped = jnp.where(chip < swapped_chips(rows), 1, 0)
+    half = (lax.axis_index("core") + swapped + (1 if for_partner else 0)) % 2
     senders = blocks_ref.shape[0]
     keep_states(count_sites(None, half, senders, capacity, sites, blocks_ref, slots_refs), out_ref)
 
@@ -173,14 +200,15 @@
 
 def merge_kernel(parts, in_ref, out_ref):
     pieces = in_ref.shape[0] // parts
+    place = places(exchange_order(in_ref.shape[0]))
     strips = in_ref.shape[1] // KMAX
     count = lax.broadcasted_iota(jnp.int32, (KMAX, LANES), 0)
     for piece in range(pieces):
         for strip in range(strips):
             rows = slice(strip * KMAX, (strip + 1) * KMAX)
-            total = in_ref[piece, rows, :]
+            total = in_ref[place[piece], rows, :]
             for part in range(1, parts):
-                other = in_ref[part * pieces + piece, rows, :]
+                other = in_ref[place[part * pieces + piece], rows, :]
                 joint = other * total[0:1, :]
                 for k in range(1, KMAX):
                     shifted = jnp.where(count >= k, pltpu.roll(other, k, 0), 0.0)
@@ -222,7 +250,22 @@
             for x in (site_cell.T, site_power[None, :], site_tile.T, shadow)
         ]
     )
-    blocks = lax.all_to_all(blocks, ("grp", "near"), split_axis=0, concat_axis=0, tiled=True)
+    gather = [
+        [
+            ((member // near * parts + far) * near + member % near) * 2 + half
+            for member in gather_order(receivers)
+        ]
+        for far in range(parts)
+        for half in (0, 1)
+    ]
+    blocks = lax.all_to_all(
+        blocks,
+        ("grp", "far", "near", "core"),
+        split_axis=0,
+        concat_axis=0,
+        axis_index_groups=gather,
+        tiled=True,
+    )
 
     dist_shape = (chips * KMAX * width // LANES, LANES)
     work = chips * width * receivers * capacity * 23
@@ -246,7 +289,18 @@
         name="join",
     )(counts(False), got)
     dist = dist.reshape(chips, KMAX * width // LANES, LANES)
-    dist = lax.all_to_all(dist, ("far", "near"), split_axis=0, concat_axis=0, tiled=True)
+    exchange = [
+        [2 * chip + (half ^ (1 if chip < swapped_chips(chips) else 0)) for chip in exchange_order(chips)]
+        for half in (0, 1)
+    ]
+    dist = lax.all_to_all(
+        dist,
+        ("far", "near", "core"),
+        split_axis=0,
+        concat_axis=0,
+        axis_index_groups=exchange,
+        tiled=True,
+    )
     return pl.pallas_call(
         functools.partial(merge_kernel, parts),
         out_shape=jax.ShapeDtypeStruct((1, KMAX, cells // groups), jnp.float32),

time: 31.7 us -> 29.4 us (0.927)
  the two profiles are of different devices: /device:TPU:0 before, /device:TPU:1 now
where the time goes in v5:
time: 29.4 us; the launch traced here: 29.2 us
  blocking collectives  24.3 us (83%)
  Pallas kernels  3.83 us (13%)
  starting transfers between devices  0.87 us (3%)
    all_to_all x1, blocking collectives, on_device(): lax.all_to_all(blocks, ('grp', 'far', 'near', 'core'), split_axis=0, conc...  13.5 us
    all_to_all x1, blocking collectives, on_device(): lax.all_to_all(dist, ('far', 'near', 'core'), split_axis=0, concat_axis=0...  10.7 us
    pallas_call x2, Pallas kernels, counts(): pl.pallas_call(functools.partial(count_kernel, for_partner, capacity, sit...  1.64 us
    pallas_call x1, Pallas kernels, on_device(): pl.pallas_call(functools.partial(probs_kernel, tiles, chips * capacity),...  1.42 us
    ppermute x1, starting transfers between devices, on_device(): got = lax.ppermute(counts(True), 'core', swap)  0.87 us
    pallas_call x1, Pallas kernels, on_device(): pl.pallas_call(functools.partial(merge_kernel, parts), out_shape=jax.Shap...  0.7 us
  transfers between devices with their start and end apart: 1, of which 1 were waited for; matrix products, arithmetic and copies ran while one was open for 0% of the time, Pallas kernels for 3%

profile of v5, /device:TPU:1, one launch (start us, length us, event | category | flops | bytes accessed | tf_op | source)
XLA Modules:
  0.0 29.2 jit_solution(4207943002252608415)
XLA Ops:
  0.0 1.4 %probs.1 = bf16[8,264,128]{2,1,0:T(8,128)(2,1)S(1)} custom-call(s32[2,64]{1,0:T(2,128)} %bitcast.5, f32[1,64]{1,0:T(1,128)} %bitcast.6, s32[1,64]{1,0:T(1,128)} %bitcast.7, bf16[64,4096]{1,0:T(8,128)(2,1)} %shadow_hbm.1), custom_call_target="tpu_custom_call" | custom-call | tf_op jit(solution)/shard_map/probs/pallas_call | solution.py:234
  1.4 13.5 %all_to_all.10.blocks_ref = bf16[8,264,128]{2,1,0:T(8,128)(2,1)S(1)} all-to-all(bf16[8,264,128]{2,1,0:T(8,128)(2,1)S(1)} %probs.1), channel_id=1, replica_groups={{22,20,18,16,6,4,2,0},{23,21,19,17,7,5,3,1},{30,28,26,24,14,12,10,8},{3..., dimensions={0} | all-to-all | bytes 1081344 | tf_op jit(solution)/shard_map/all_to_all | solution.py:261
  14.9 0.8 %counts_partner.1 = f32[256,128]{1,0:T(8,128)S(1)} custom-call(bf16[8,264,128]{2,1,0:T(8,128)(2,1)S(1)} %all_to_all.10.blocks_ref), custom_call_target="tpu_custom_call" | custom-call | flops 6029312 | bytes 1048576 | tf_op jit(solution)/shard_map/counts_partner/pallas_call | solution.py:274
  15.8 0.9 %collective-permute-start = (f32[256,128]{1,0:T(8,128)S(1)}, f32[256,128]{1,0:T(8,128)S(1)}, u32[]{:S(2)}, u32[]{:S(2)}) collective-permute-start(f32[256,128]{1,0:T(8,128)S(1)} %counts_partner.1), channel_id=1, source_target_pairs={{0,1},{1,0},{2,3},{3,2},{4,5},{5,4},{6,7},{7,6},{8,9},{9,8},{10,11... | collective-permute-start | bytes 393224 | tf_op jit(solution)/shard_map/ppermute | solution.py:284
  16.6 0.8 %counts_own.1.own_ref = f32[256,128]{1,0:T(8,128)S(1)} custom-call(bf16[8,264,128]{2,1,0:T(8,128)(2,1)S(1)} %all_to_all.10.blocks_ref), custom_call_target="tpu_custom_call" | custom-call | flops 6029312 | bytes 1048576 | tf_op jit(solution)/shard_map/counts_own/pallas_call | solution.py:274
  17.5 0.2 collective-permute-done.got_ref
  17.6 0.1 join.1
  17.7 10.7 %all_to_all.11.in_ref = f32[8,32,128]{2,1,0:T(8,128)S(1)} all-to-all(f32[8,32,128]{2,1,0:T(8,128)S(1)} %bitcast.4), channel_id=1, replica_groups={{8,10,14,12,5,7,3,1},{9,11,15,13,4,6,2,0},{24,26,30,28,21,23,19,17},{25..., dimensions={0} | all-to-all | bytes 262144 | tf_op jit(solution)/shard_map/all_to_all | solution.py:296
  28.5 0.7 %merge.1 = f32[1,8,2048]{2,1,0:T(8,128)} custom-call(f32[8,32,128]{2,1,0:T(8,128)S(1)} %all_to_all.11.in_ref), custom_call_target="tpu_custom_call" | custom-call | tf_op jit(solution)/shard_map/merge/pallas_call | solution.py:304
Async XLA Ops:
  15.8 1.9 %collective-permute-start = (f32[256,128]{1,0:T(8,128)S(1)}, f32[256,128]{1,0:T(8,128)S(1)}, u32[]{:S(2)}, u32[]{:S(2)}) collective-permute-start(f32[256,128]{1,0:T(8,128)S(1)} %counts_partner.1), channel_id=1, source_target_pairs={{0,1},{1,0},{2,3},{3,2},{4,5},{5,4},{6,7},{7,6},{8,9},{9,8},{10,11... | collective-permute-start | bytes 393224 | tf_op jit(solution)/shard_map/ppermute | solution.py:284

commit v6 on v5

--- a/solution.py
+++ b/solution.py
@@ -19,16 +19,16 @@
     return chips // 2
 
 
-def backwards(count):
-    return list(range(count))[::-1]
-
-
-def gray_backwards(count):
-    return [i ^ (i >> 1) for i in range(count)][::-1]
-
-
-gather_order = backwards
-exchange_order = gray_backwards
+GATHER_ORDER = (6, 7, 2, 4, 0, 3, 1, 5)
+EXCHANGE_ORDER = (4, 2, 5, 1, 0, 7, 3, 6)
+
+
+def gather_order(count):
+    return list(GATHER_ORDER) if count == len(GATHER_ORDER) else list(range(count))[::-1]
+
+
+def exchange_order(count):
+    return list(EXCHANGE_ORDER) if count == len(EXCHANGE_ORDER) else list(range(count))[::-1]
 
 
 def places(order):

time: 29.4 us -> 27.7 us (0.942)
  the two profiles are of different devices: /device:TPU:1 before, /device:TPU:0 now
where the time goes in v6:
time: 27.7 us; the launch traced here: 27.4 us
  blocking collectives  22.9 us (83%)
  Pallas kernels  3.83 us (14%)
  waiting for transfers between devices  0.5 us (2%)
    all_to_all x1, blocking collectives, on_device(): lax.all_to_all(blocks, ('grp', 'far', 'near', 'core'), split_axis=0, conc...  14.2 us
    all_to_all x1, blocking collectives, on_device(): lax.all_to_all(dist, ('far', 'near', 'core'), split_axis=0, concat_axis=0...  8.7 us
    pallas_call x2, Pallas kernels, counts(): pl.pallas_call(functools.partial(count_kernel, for_partner, capacity, sit...  1.64 us
    pallas_call x1, Pallas kernels, on_device(): pl.pallas_call(functools.partial(probs_kernel, tiles, chips * capacity),...  1.42 us
    pallas_call x1, Pallas kernels, on_device(): pl.pallas_call(functools.partial(merge_kernel, parts), out_shape=jax.Shap...  0.7 us
  transfers between devices with their start and end apart: 1, of which 1 were waited for; matrix products, arithmetic and copies ran while one was open for 0% of the time, Pallas kernels for 3%

profile of v6, /device:TPU:0, one launch (start us, length us, event | category | flops | bytes accessed | tf_op | source)
XLA Modules:
  0.0 27.4 jit_solution(101759062734202740)
XLA Ops:
  0.0 1.4 %probs.1 = bf16[8,264,128]{2,1,0:T(8,128)(2,1)S(1)} custom-call(s32[2,64]{1,0:T(2,128)} %bitcast.5, f32[1,64]{1,0:T(1,128)} %bitcast.6, s32[1,64]{1,0:T(1,128)} %bitcast.7, bf16[64,4096]{1,0:T(8,128)(2,1)} %shadow_hbm.1), custom_call_target="tpu_custom_call" | custom-call | tf_op jit(solution)/shard_map/probs/pallas_call | solution.py:234
  1.4 14.2 %all_to_all.10.blocks_ref = bf16[8,264,128]{2,1,0:T(8,128)(2,1)S(1)} all-to-all(bf16[8,264,128]{2,1,0:T(8,128)(2,1)S(1)} %probs.1), channel_id=1, replica_groups={{20,22,4,16,0,6,2,18},{21,23,5,17,1,7,3,19},{28,30,12,24,8,14,10,26},{2..., dimensions={0} | all-to-all | bytes 1081344 | tf_op jit(solution)/shard_map/all_to_all | solution.py:261
  15.6 0.8 %counts_partner.1 = f32[256,128]{1,0:T(8,128)S(1)} custom-call(bf16[8,264,128]{2,1,0:T(8,128)(2,1)S(1)} %all_to_all.10.blocks_ref), custom_call_target="tpu_custom_call" | custom-call | flops 6029312 | bytes 1048576 | tf_op jit(solution)/shard_map/counts_partner/pallas_call | solution.py:274
  16.5 0.1 collective-permute-start
  16.5 0.8 %counts_own.1.own_ref = f32[256,128]{1,0:T(8,128)S(1)} custom-call(bf16[8,264,128]{2,1,0:T(8,128)(2,1)S(1)} %all_to_all.10.blocks_ref), custom_call_target="tpu_custom_call" | custom-call | flops 6029312 | bytes 1048576 | tf_op jit(solution)/shard_map/counts_own/pallas_call | solution.py:274
  17.4 0.5 %collective-permute-done.got_ref = f32[256,128]{1,0:T(8,128)S(1)} collective-permute-done((f32[256,128]{1,0:T(8,128)S(1)}, f32[256,128]{1,0:T(8,128)S(1)}, u32[]{:S(2)}, u32[]{:S(2)}) %collective-permute-start) | collective-permute-done | bytes 131104 | tf_op jit(solution)/shard_map/ppermute | solution.py:284
  17.9 0.1 join.1
  18.0 8.7 %all_to_all.11.in_ref = f32[8,32,128]{2,1,0:T(8,128)S(1)} all-to-all(f32[8,32,128]{2,1,0:T(8,128)S(1)} %bitcast.4), channel_id=1, replica_groups={{8,5,10,3,1,14,7,12},{9,4,11,2,0,15,6,13},{24,21,26,19,17,30,23,28},{25..., dimensions={0} | all-to-all | bytes 262144 | tf_op jit(solution)/shard_map/all_to_all | solution.py:296
  26.7 0.7 %merge.1 = f32[1,8,2048]{2,1,0:T(8,128)} custom-call(f32[8,32,128]{2,1,0:T(8,128)S(1)} %all_to_all.11.in_ref), custom_call_target="tpu_custom_call" | custom-call | tf_op jit(solution)/shard_map/merge/pallas_call | solution.py:304
Async XLA Ops:
  16.5 1.4 %collective-permute-start = (f32[256,128]{1,0:T(8,128)S(1)}, f32[256,128]{1,0:T(8,128)S(1)}, u32[]{:S(2)}, u32[]{:S(2)}) collective-permute-start(f32[256,128]{1,0:T(8,128)S(1)} %counts_partner.1), channel_id=1, source_target_pairs={{0,1},{1,0},{2,3},{3,2},{4,5},{5,4},{6,7},{7,6},{8,9},{9,8},{10,11... | collective-permute-start | bytes 393224 | tf_op jit(solution)/shard_map/ppermute | solution.py:284

commit v7 on v6

--- a/solution.py
+++ b/solution.py
@@ -19,8 +19,8 @@
     return chips // 2
 
 
-GATHER_ORDER = (6, 7, 2, 4, 0, 3, 1, 5)
-EXCHANGE_ORDER = (4, 2, 5, 1, 0, 7, 3, 6)
+GATHER_ORDER = (6, 7, 2, 3, 0, 4, 1, 5)
+EXCHANGE_ORDER = (4, 2, 5, 6, 0, 7, 3, 1)
 
 
 def gather_order(count):

time: 27.7 us -> 27.7 us (level)
  no operation moved by 1% of the time
where the time goes in v7:
time: 27.7 us; the launch traced here: 27.4 us
  blocking collectives  22.9 us (83%)
  Pallas kernels  3.83 us (14%)
  waiting for transfers between devices  0.5 us (2%)
    all_to_all x1, blocking collectives, on_device(): lax.all_to_all(blocks, ('grp', 'far', 'near', 'core'), split_axis=0, conc...  14.2 us
    all_to_all x1, blocking collectives, on_device(): lax.all_to_all(dist, ('far', 'near', 'core'), split_axis=0, concat_axis=0...  8.7 us
    pallas_call x2, Pallas kernels, counts(): pl.pallas_call(functools.partial(count_kernel, for_partner, capacity, sit...  1.63 us
    pallas_call x1, Pallas kernels, on_device(): pl.pallas_call(functools.partial(probs_kernel, tiles, chips * capacity),...  1.42 us
    pallas_call x1, Pallas kernels, on_device(): pl.pallas_call(functools.partial(merge_kernel, parts), out_shape=jax.Shap...  0.7 us
  transfers between devices with their start and end apart: 1, of which 1 were waited for; matrix products, arithmetic and copies ran while one was open for 0% of the time, Pallas kernels for 3%

profile of v7, /device:TPU:0, one launch (start us, length us, event | category | flops | bytes accessed | tf_op | source)
XLA Modules:
  0.0 27.4 jit_solution(13173999339174793325)
XLA Ops:
  0.0 1.4 %probs.1 = bf16[8,264,128]{2,1,0:T(8,128)(2,1)S(1)} custom-call(s32[2,64]{1,0:T(2,128)} %bitcast.5, f32[1,64]{1,0:T(1,128)} %bitcast.6, s32[1,64]{1,0:T(1,128)} %bitcast.7, bf16[64,4096]{1,0:T(8,128)(2,1)} %shadow_hbm.1), custom_call_target="tpu_custom_call" | custom-call | tf_op jit(solution)/shard_map/probs/pallas_call | solution.py:234
  1.4 14.2 %all_to_all.10.blocks_ref = bf16[8,264,128]{2,1,0:T(8,128)(2,1)S(1)} all-to-all(bf16[8,264,128]{2,1,0:T(8,128)(2,1)S(1)} %probs.1), channel_id=1, replica_groups={{20,22,4,6,0,16,2,18},{21,23,5,7,1,17,3,19},{28,30,12,14,8,24,10,26},{2..., dimensions={0} | all-to-all | bytes 1081344 | tf_op jit(solution)/shard_map/all_to_all | solution.py:261
  15.7 0.8 %counts_partner.1 = f32[256,128]{1,0:T(8,128)S(1)} custom-call(bf16[8,264,128]{2,1,0:T(8,128)(2,1)S(1)} %all_to_all.10.blocks_ref), custom_call_target="tpu_custom_call" | custom-call | flops 6029312 | bytes 1048576 | tf_op jit(solution)/shard_map/counts_partner/pallas_call | solution.py:274
  16.5 0.1 collective-permute-start
  16.5 0.8 %counts_own.1.own_ref = f32[256,128]{1,0:T(8,128)S(1)} custom-call(bf16[8,264,128]{2,1,0:T(8,128)(2,1)S(1)} %all_to_all.10.blocks_ref), custom_call_target="tpu_custom_call" | custom-call | flops 6029312 | bytes 1048576 | tf_op jit(solution)/shard_map/counts_own/pallas_call | solution.py:274
  17.4 0.5 %collective-permute-done.got_ref = f32[256,128]{1,0:T(8,128)S(1)} collective-permute-done((f32[256,128]{1,0:T(8,128)S(1)}, f32[256,128]{1,0:T(8,128)S(1)}, u32[]{:S(2)}, u32[]{:S(2)}) %collective-permute-start) | collective-permute-done | bytes 131104 | tf_op jit(solution)/shard_map/ppermute | solution.py:284
  17.9 0.1 join.1
  18.0 8.7 %all_to_all.11.in_ref = f32[8,32,128]{2,1,0:T(8,128)S(1)} all-to-all(f32[8,32,128]{2,1,0:T(8,128)S(1)} %bitcast.4), channel_id=1, replica_groups={{8,5,10,12,1,14,7,3},{9,4,11,13,0,15,6,2},{24,21,26,28,17,30,23,19},{25..., dimensions={0} | all-to-all | bytes 262144 | tf_op jit(solution)/shard_map/all_to_all | solution.py:296
  26.7 0.7 %merge.1 = f32[1,8,2048]{2,1,0:T(8,128)} custom-call(f32[8,32,128]{2,1,0:T(8,128)S(1)} %all_to_all.11.in_ref), custom_call_target="tpu_custom_call" | custom-call | tf_op jit(solution)/shard_map/merge/pallas_call | solution.py:304
Async XLA Ops:
  16.5 1.4 %collective-permute-start = (f32[256,128]{1,0:T(8,128)S(1)}, f32[256,128]{1,0:T(8,128)S(1)}, u32[]{:S(2)}, u32[]{:S(2)}) collective-permute-start(f32[256,128]{1,0:T(8,128)S(1)} %counts_partner.1), channel_id=1, source_target_pairs={{0,1},{1,0},{2,3},{3,2},{4,5},{5,4},{6,7},{7,6},{8,9},{9,8},{10,11... | collective-permute-start | bytes 393224 | tf_op jit(solution)/shard_map/ppermute | solution.py:284
